TPU v7x, 128 devices: a whole 4x4x4 slice. The times are simulated.
128 devices in a mesh: gx: 8 (over y_lo, z), gy: 16 (over y_hi, x, core).
Axes of the slice: x: 4, y: 4 (y_hi: 2, y_lo: 2; y = y_hi * 2 + y_lo), z: 4, core: 2. Of those that a mesh axis runs over, the one named last changes fastest.
Arguments:
- thickness: float32 [4096, 2048], P('gy', 'gx'), may hold values from 0.5 to 2
- driving: float32 [2, 4096, 2048], P(None, 'gy', 'gx'), may hold values from -6 to 6
- observed: float32 [2, 4096, 2048], P(None, 'gy', 'gx'), may hold values from -2 to 2
- control: float32 [64, 4096], P('gy'), may hold values from 0.5 to 1.5
- ice_mask: int32 [16, 8], replicated, may hold values 0 or 1
- tile_block: int32 [16, 8, 1], replicated, may hold values from 0 to 63
Outputs:
- vel_u: float32 [4096, 2048], P('gy', 'gx')
- vel_v: float32 [4096, 2048], P('gy', 'gx')
- grad_control: float32 [64, 4096], P('gy')
Inputs may be any that keep to these rules, and one draw needn't show every extreme that they name: `tile_block`: every one of the 64 control blocks is named by at least one tile.
All inputs are finite; a program needn't handle non-finite values.
Results may differ from a plain program's by a relative error of at most 0.00015.
Values sent between devices are 32-bit elements; how exact they have to be, the bound alone decides.
A program may use at most 64 MiB of HBM per device.

v0:
```python
import jax
import jax.numpy as jnp
from jax import lax
from jax.sharding import PartitionSpec as P

TILE = 256
CPC = 4
PIC = 4
SW = 2
ADJ = 6
CT = 64
COARSE = 4096
visc_scale = 0.1
strain_floor = 0.05


def with_halo(cells, sides, width):
    for axis, dim in sides:
        count = lax.axis_size(axis)
        ends = count - 1
        head = lax.slice_in_dim(cells, 0, width, axis=dim)
        tail = lax.slice_in_dim(cells, cells.shape[dim] - width, cells.shape[dim], axis=dim)
        cells = jnp.concatenate(
            [
                lax.ppermute(tail, axis, [(i, (i + 1) % count) for i in range(ends)]),
                cells,
                lax.ppermute(head, axis, [((i + 1) % count, i) for i in range(ends)]),
            ],
            axis=dim,
        )
    return cells


def viscosity(vel_pad, thick):
    speed_x = vel_pad[0]
    speed_y = vel_pad[1]
    dudx = 0.5 * (speed_x[1:-1, 2:] - speed_x[1:-1, :-2])
    dudy = 0.5 * (speed_x[2:, 1:-1] - speed_x[:-2, 1:-1])
    dvdx = 0.5 * (speed_y[1:-1, 2:] - speed_y[1:-1, :-2])
    dvdy = 0.5 * (speed_y[2:, 1:-1] - speed_y[:-2, 1:-1])
    shear = dudy + dvdx
    strain = dudx * dudx + dvdy * dvdy + dudx * dvdy + 0.25 * shear * shear + strain_floor
    return visc_scale * thick * jnp.power(strain, -1.0 / 3.0)


def coefficients(visc_pad, friction):
    center = visc_pad[1:-1, 1:-1]
    east_w = 0.5 * (center + visc_pad[1:-1, 2:])
    west_w = 0.5 * (center + visc_pad[1:-1, :-2])
    south_w = 0.5 * (center + visc_pad[2:, 1:-1])
    north_w = 0.5 * (center + visc_pad[:-2, 1:-1])
    diag_u = friction + 4.0 * (east_w + west_w) + south_w + north_w
    diag_v = friction + east_w + west_w + 4.0 * (south_w + north_w)
    return (visc_pad, east_w, west_w, south_w, north_w, diag_u, diag_v)


def relaxation(vel_pad, stencil_coef, forcing, ice_cells):
    visc_pad, east_w, west_w, south_w, north_w, diag_u, diag_v = stencil_coef
    speed_x = vel_pad[0]
    speed_y = vel_pad[1]
    flux_p = 2.0 * visc_pad[1:-1, :] * (0.5 * (speed_y[2:, :] - speed_y[:-2, :]))
    flux_q = visc_pad[:, 1:-1] * (0.5 * (speed_y[:, 2:] - speed_y[:, :-2]))
    cross_u = 0.5 * (flux_p[:, 2:] - flux_p[:, :-2]) + 0.5 * (flux_q[2:, :] - flux_q[:-2, :])
    flux_r = 2.0 * visc_pad[:, 1:-1] * (0.5 * (speed_x[:, 2:] - speed_x[:, :-2]))
    flux_s = visc_pad[1:-1, :] * (0.5 * (speed_x[2:, :] - speed_x[:-2, :]))
    cross_v = 0.5 * (flux_r[2:, :] - flux_r[:-2, :]) + 0.5 * (flux_s[:, 2:] - flux_s[:, :-2])
    near_u = (
        4.0 * (east_w * speed_x[1:-1, 2:] + west_w * speed_x[1:-1, :-2])
        + south_w * speed_x[2:, 1:-1]
        + north_w * speed_x[:-2, 1:-1]
    )
    near_v = (
        east_w * speed_y[1:-1, 2:]
        + west_w * speed_y[1:-1, :-2]
        + 4.0 * (south_w * speed_y[2:, 1:-1] + north_w * speed_y[:-2, 1:-1])
    )
    new_u = ice_cells * (forcing[0] + near_u + cross_u) / diag_u
    new_v = ice_cells * (forcing[1] + near_v + cross_v) / diag_v
    return jnp.stack([new_u, new_v])


def halo_velocity(field):
    return with_halo(field, (("gx", 2), ("gy", 1)), 1)


def per_device(thickness, driving, observed, control, ice_mask, tile_block):
    row_count, col_count = thickness.shape
    tile_count = col_count // TILE
    owned_rows = control.shape[0]
    row_tile = lax.axis_index("gy")
    col_tile = lax.axis_index("gx") * tile_count
    blocks = lax.dynamic_slice(tile_block[:, :, 0], (row_tile, col_tile), (1, tile_count))[0]
    ice_tiles = lax.dynamic_slice(ice_mask, (row_tile, col_tile), (1, tile_count))[0].astype(
        jnp.float32
    )
    ice_cells = jnp.broadcast_to(ice_tiles[None, :, None], (TILE, tile_count, TILE)).reshape(
        row_count, col_count
    )
    rates = jnp.exp(control)
    shard_rows = lax.all_gather(rates, "gy", axis=0, tiled=True)
    labels = jnp.arange(shard_rows.shape[0], dtype=jnp.int32)
    onehot = (blocks[:, None] == labels[None, :]).astype(jnp.float32)
    picked = jnp.dot(onehot, shard_rows, precision=lax.Precision.HIGHEST)
    friction = jnp.broadcast_to(
        picked.reshape(tile_count, CT, 1, CT, 1), (tile_count, CT, CPC, CT, CPC)
    )
    friction = (
        friction.reshape(tile_count, TILE, TILE).transpose(1, 0, 2).reshape(row_count, col_count)
    )
    velocity = jnp.zeros((2, row_count, col_count), jnp.float32)
    stencil_coef = None
    for picard in range(PIC):
        vel_pad = halo_velocity(velocity)
        visc_cells = viscosity(vel_pad, thickness)
        visc_pad = with_halo(visc_cells, (("gx", 1), ("gy", 0)), 1)
        stencil_coef = coefficients(visc_pad, friction)
        for sweep in range(SW):
            if sweep > 0:
                vel_pad = halo_velocity(velocity)
            velocity = relaxation(vel_pad, stencil_coef, driving, ice_cells)
    misfit = ice_cells * (velocity - observed)
    adjoint = jnp.zeros((2, row_count, col_count), jnp.float32)
    for sweep in range(ADJ):
        adjoint = relaxation(halo_velocity(adjoint), stencil_coef, misfit, ice_cells)
    cell_grad = -friction * (velocity[0] * adjoint[0] + velocity[1] * adjoint[1])
    tile_grad = cell_grad.reshape(CT, CPC, tile_count, CT, CPC).sum(axis=(1, 4))
    tile_grad = tile_grad.transpose(1, 0, 2).reshape(tile_count, COARSE)
    labels = jnp.arange(owned_rows * lax.axis_size("gy"), dtype=jnp.int32)
    onehot = (labels[:, None] == blocks[None, :]).astype(jnp.float32)
    partial_sum = lax.psum_scatter(
        jnp.dot(onehot, tile_grad, precision=lax.Precision.HIGHEST),
        "gy",
        scatter_dimension=0,
        tiled=True,
    )
    gradient = lax.psum(partial_sum, "gx")
    return (velocity[0], velocity[1], gradient)


def solution(mesh):
    return jax.shard_map(
        per_device,
        mesh=mesh,
        in_specs=(P("gy", "gx"), P(None, "gy", "gx"), P(None, "gy", "gx"), P("gy", None), P(), P()),
        out_specs=(P("gy", "gx"), P("gy", "gx"), P("gy", None)),
        check_vma=False,
    )
```

profile of v0, /device:TPU:0, one launch (start us, length us, event | category | flops | bytes accessed | tf_op | source)
XLA Modules:
  0.0 709.3 jit_solution(17794844136733789249)
XLA Ops:
  8.6 4.6 collective-permute-start
  14.7 2.8 collective-permute-done.1
  20.1 3.0 collective-permute-start.2
  26.5 5.0 collective-permute-start.5
  37.8 3.0 collective-permute-start.7
  44.4 19.9 %all-gather.3.cloned.1.call-done = f32[16,4,4096]{2,1,0:T(4,128)} async-done(((f32[1,4,4096]{2,1,0:T(4,128)}), f32[16,4,4096]{2,1,0:T(4,128)}) %all-gather.3.cloned.1.call-update) | async-done | bytes 1048592 | tf_op jit(solution)/shard_map/all_gather | solution.py:100
  64.3 2.6 reshape.217
  66.9 3.1 reshape.211
  70.0 4.0 fusion
  74.0 4.0 broadcast_in_dim.7
  78.0 8.4 %broadcast_in_dim.8 = f32[256,256]{1,0:T(8,128)S(1)} reshape(f32[64,4,64,4]{3,2,1,0:T(8,128)} %broadcast_in_dim.7) | data formatting | bytes 524288 | tf_op jit(solution)/shard_map/broadcast_in_dim | solution.py:104
  86.4 2.1 fusion.435
  90.5 4.7 collective-permute-start.8
  95.2 4.4 collective-permute-done.9
  102.3 3.2 collective-permute-start.10
  110.1 5.2 collective-permute-start.12
  115.3 5.0 collective-permute-done.13
  123.1 3.0 collective-permute-start.14
  129.5 5.0 collective-permute-start.17
  134.5 2.1 collective-permute-done.16
  140.1 3.0 collective-permute-start.19
  146.9 5.0 collective-permute-start.20
  151.9 4.4 collective-permute-done.21
  156.3 1.8 collective-permute-done.20
  159.5 3.1 collective-permute-start.22
  167.4 6.2 collective-permute-start.24
  173.5 4.2 collective-permute-done.25
  177.7 1.8 collective-permute-done.24
  180.9 3.4 collective-permute-start.26
  187.6 7.1 %collective-permute-start.29 = (f32[256,1]{1,0:T(8,128)S(1)}, f32[256,1]{1,0:T(8,128)S(1)}, u32[]{:S(2)}, u32[]{:S(2)}) collective-permute-start(f32[256,1]{1,0:T(8,128)S(1)} %get-tuple-element.142), channel_id=1, source_target_pairs={{0,16},{16,32},{32,48},{48,64},{64,80},{80,96},{96,112},{1,17},{17... | collective-permute-start | bytes 3080 | tf_op jit(solution)/shard_map/ppermute | solution.py:25
  199.0 4.3 collective-permute-start.31
  206.9 7.1 %collective-permute-start.32 = (f32[2,256,1]{2,1,0:T(8,128)S(1)}, f32[2,256,1]{2,1,0:T(8,128)S(1)}, u32[]{:S(2)}, u32[]{:S(2)}) collective-permute-start(f32[2,256,1]{2,1,0:T(8,128)S(1)} %get-tuple-element.99), channel_id=1, source_target_pairs={{0,16},{16,32},{32,48},{48,64},{64,80},{80,96},{96,112},{1,17},{17... | collective-permute-start | bytes 6152 | tf_op jit(solution)/shard_map/ppermute | solution.py:25
  214.0 2.8 collective-permute-done.33
  216.8 1.7 collective-permute-done.32
  219.9 4.8 collective-permute-start.34
  229.5 7.1 %collective-permute-start.36 = (f32[2,256,1]{2,1,0:T(8,128)S(1)}, f32[2,256,1]{2,1,0:T(8,128)S(1)}, u32[]{:S(2)}, u32[]{:S(2)}) collective-permute-start(f32[2,256,1]{2,1,0:T(8,128)S(1)} %get-tuple-element.97), channel_id=1, source_target_pairs={{0,16},{16,32},{32,48},{48,64},{64,80},{80,96},{96,112},{1,17},{17... | collective-permute-start | bytes 6152 | tf_op jit(solution)/shard_map/ppermute | solution.py:25
  236.6 2.4 collective-permute-done.37
  241.9 5.5 collective-permute-start.38
  250.6 7.1 %collective-permute-start.41 = (f32[256,1]{1,0:T(8,128)S(1)}, f32[256,1]{1,0:T(8,128)S(1)}, u32[]{:S(2)}, u32[]{:S(2)}) collective-permute-start(f32[256,1]{1,0:T(8,128)S(1)} %get-tuple-element.140), channel_id=1, source_target_pairs={{0,16},{16,32},{32,48},{48,64},{64,80},{80,96},{96,112},{1,17},{17... | collective-permute-start | bytes 3080 | tf_op jit(solution)/shard_map/ppermute | solution.py:25
  262.1 5.2 collective-permute-start.43
  271.0 7.1 %collective-permute-start.44 = (f32[2,256,1]{2,1,0:T(8,128)S(1)}, f32[2,256,1]{2,1,0:T(8,128)S(1)}, u32[]{:S(2)}, u32[]{:S(2)}) collective-permute-start(f32[2,256,1]{2,1,0:T(8,128)S(1)} %get-tuple-element.95), channel_id=1, source_target_pairs={{0,16},{16,32},{32,48},{48,64},{64,80},{80,96},{96,112},{1,17},{17... | collective-permute-start | bytes 6152 | tf_op jit(solution)/shard_map/ppermute | solution.py:25
  278.2 2.8 collective-permute-done.45
  284.1 5.2 collective-permute-start.46
  295.4 7.1 %collective-permute-start.48 = (f32[2,256,1]{2,1,0:T(8,128)S(1)}, f32[2,256,1]{2,1,0:T(8,128)S(1)}, u32[]{:S(2)}, u32[]{:S(2)}) collective-permute-start(f32[2,256,1]{2,1,0:T(8,128)S(1)} %get-tuple-element.93), channel_id=1, source_target_pairs={{0,16},{16,32},{32,48},{48,64},{64,80},{80,96},{96,112},{1,17},{17... | collective-permute-start | bytes 6152 | tf_op jit(solution)/shard_map/ppermute | solution.py:25
  302.6 2.8 collective-permute-done.49
  305.4 1.7 collective-permute-done.48
  308.5 4.8 collective-permute-start.50
  317.9 7.1 %collective-permute-start.52 = (f32[2,256,1]{2,1,0:T(8,128)S(1)}, f32[2,256,1]{2,1,0:T(8,128)S(1)}, u32[]{:S(2)}, u32[]{:S(2)}) collective-permute-start(f32[2,256,1]{2,1,0:T(8,128)S(1)} %get-tuple-element.91), channel_id=1, source_target_pairs={{0,16},{16,32},{32,48},{48,64},{64,80},{80,96},{96,112},{1,17},{17... | collective-permute-start | bytes 6152 | tf_op jit(solution)/shard_map/ppermute | solution.py:25
  325.0 3.2 collective-permute-done.53
  331.4 4.3 collective-permute-start.54
  340.3 6.8 collective-permute-start.56
  347.1 2.4 collective-permute-done.57
  352.3 6.1 collective-permute-start.58
  363.0 7.1 %collective-permute-start.60 = (f32[2,256,1]{2,1,0:T(8,128)S(1)}, f32[2,256,1]{2,1,0:T(8,128)S(1)}, u32[]{:S(2)}, u32[]{:S(2)}) collective-permute-start(f32[2,256,1]{2,1,0:T(8,128)S(1)} %get-tuple-element.87), channel_id=1, source_target_pairs={{0,16},{16,32},{32,48},{48,64},{64,80},{80,96},{96,112},{1,17},{17... | collective-permute-start | bytes 6152 | tf_op jit(solution)/shard_map/ppermute | solution.py:25
  370.2 2.4 collective-permute-done.61
  375.4 8.5 %collective-permute-start.62 = (f32[2,1,258]{2,1,0:T(1,128)S(1)}, f32[2,1,258]{2,1,0:T(1,128)S(1)}, u32[]{:S(2)}, u32[]{:S(2)}) collective-permute-start(f32[2,1,258]{2,1,0:T(1,128)S(1)} %get-tuple-element.36), channel_id=1, source_target_pairs={{0,1},{1,2},{2,3},{3,4},{4,5},{5,6},{6,7},{7,8},{8,9},{9,10},{10,1... | collective-permute-start | bytes 6200 | tf_op jit(solution)/shard_map/ppermute | solution.py:25
  388.3 7.1 %collective-permute-start.64 = (f32[2,256,1]{2,1,0:T(8,128)S(1)}, f32[2,256,1]{2,1,0:T(8,128)S(1)}, u32[]{:S(2)}, u32[]{:S(2)}) collective-permute-start(f32[2,256,1]{2,1,0:T(8,128)S(1)} %get-tuple-element.85), channel_id=1, source_target_pairs={{0,16},{16,32},{32,48},{48,64},{64,80},{80,96},{96,112},{1,17},{17... | collective-permute-start | bytes 6152 | tf_op jit(solution)/shard_map/ppermute | solution.py:25
  395.5 2.4 collective-permute-done.65
  399.4 7.7 %collective-permute-start.66 = (f32[2,1,258]{2,1,0:T(1,128)S(1)}, f32[2,1,258]{2,1,0:T(1,128)S(1)}, u32[]{:S(2)}, u32[]{:S(2)}) collective-permute-start(f32[2,1,258]{2,1,0:T(1,128)S(1)} %get-tuple-element.34), channel_id=1, source_target_pairs={{0,1},{1,2},{2,3},{3,4},{4,5},{5,6},{6,7},{7,8},{8,9},{9,10},{10,1... | collective-permute-start | bytes 6200 | tf_op jit(solution)/shard_map/ppermute | solution.py:25
  409.0 7.8 %collective-permute-done.67 = f32[2,1,258]{2,1,0:T(1,128)S(1)} collective-permute-done((f32[2,1,258]{2,1,0:T(1,128)S(1)}, f32[2,1,258]{2,1,0:T(1,128)S(1)}, u32[]{:S(2)}, u32[]{:S(2)}) %collective-permute-start.67) | collective-permute-done | bytes 2096 | tf_op jit(solution)/shard_map/ppermute | solution.py:27
  419.0 10.1 %reshape.213 = f32[64,4,64,4]{3,2,1,0:T(8,128)} reshape(f32[256,256]{1,0:T(8,128)S(1)} %fusion.161) | data formatting | bytes 524288 | tf_op jit(solution)/shard_map/reshape | solution.py:126
  429.1 4.1 reduce_sum.9
  435.7 188.1 %all-reduce.6.cloned.1.call-done = f32[64,4096]{1,0:T(8,128)} async-done(((f32[64,4096]{1,0:T(8,128)}), f32[64,4096]{1,0:T(8,128)}) %all-reduce.6.cloned.1.call-update) | async-done | bytes 1048592
  625.4 75.7 %all-reduce.4.cloned.1.call-done = f32[4,4096]{1,0:T(4,128)} async-done(((f32[4,4096]{1,0:T(4,128)}), f32[4,4096]{1,0:T(4,128)}) %all-reduce.4.cloned.1.call-update) | async-done | bytes 65552 | tf_op jit(solution)/shard_map/psum | solution.py:136
  (264 shorter events, 126.8 us)
Async XLA Ops:
  7.2 57.2 %all-gather.3.cloned.1.call-start = ((), (), s32[]{:S(2)}) async-start(), calls=%async_computation.1 | async-start | bytes 1114112 | tf_op jit(solution)/shard_map/all_gather | solution.py:100
  7.3 10.2 %collective-permute-start.1 = (f32[2,256,1]{2,1,0:T(8,128)S(1)}, f32[2,256,1]{2,1,0:T(8,128)S(1)}, u32[]{:S(2)}, u32[]{:S(2)}) collective-permute-start(f32[2,256,1]{2,1,0:T(8,128)S(1)} %broadcast.112), channel_id=1, source_target_pairs={{16,0},{32,16},{48,32},{64,48},{80,64},{96,80},{112,96},{17,1},{33... | collective-permute-start | bytes 6152 | tf_op jit(solution)/shard_map/ppermute | solution.py:27
  8.6 10.1 %collective-permute-start = (f32[2,256,1]{2,1,0:T(8,128)S(1)}, f32[2,256,1]{2,1,0:T(8,128)S(1)}, u32[]{:S(2)}, u32[]{:S(2)}) collective-permute-start(f32[2,256,1]{2,1,0:T(8,128)S(1)} %broadcast.112), channel_id=1, source_target_pairs={{0,16},{16,32},{32,48},{48,64},{64,80},{80,96},{96,112},{1,17},{17... | collective-permute-start | bytes 6152 | tf_op jit(solution)/shard_map/ppermute | solution.py:25
  14.6 609.2 %all-reduce.6.cloned.1.call-start = ((), (), s32[]{:S(2)}) async-start(), calls=%async_computation.2 | async-start | bytes 2097152
  18.8 4.3 collective-permute-start.3
  25.2 8.9 %collective-permute-start.4 = (f32[256,1]{1,0:T(8,128)S(1)}, f32[256,1]{1,0:T(8,128)S(1)}, u32[]{:S(2)}, u32[]{:S(2)}) collective-permute-start(f32[256,1]{1,0:T(8,128)S(1)} %get-tuple-element.147), channel_id=1, source_target_pairs={{16,0},{32,16},{48,32},{64,48},{80,64},{96,80},{112,96},{17,1},{33... | collective-permute-start | bytes 3080 | tf_op jit(solution)/shard_map/ppermute | solution.py:27
  26.5 8.8 %collective-permute-start.5 = (f32[256,1]{1,0:T(8,128)S(1)}, f32[256,1]{1,0:T(8,128)S(1)}, u32[]{:S(2)}, u32[]{:S(2)}) collective-permute-start(f32[256,1]{1,0:T(8,128)S(1)} %get-tuple-element.146), channel_id=1, source_target_pairs={{0,16},{16,32},{32,48},{48,64},{64,80},{80,96},{96,112},{1,17},{17... | collective-permute-start | bytes 3080 | tf_op jit(solution)/shard_map/ppermute | solution.py:25
  36.5 5.4 collective-permute-start.6
  89.2 10.4 %collective-permute-start.9 = (f32[2,256,1]{2,1,0:T(8,128)S(1)}, f32[2,256,1]{2,1,0:T(8,128)S(1)}, u32[]{:S(2)}, u32[]{:S(2)}) collective-permute-start(f32[2,256,1]{2,1,0:T(8,128)S(1)} %get-tuple-element.108), channel_id=1, source_target_pairs={{16,0},{32,16},{48,32},{64,48},{80,64},{96,80},{112,96},{17,1},{33... | collective-permute-start | bytes 6152 | tf_op jit(solution)/shard_map/ppermute | solution.py:27
  90.5 10.4 %collective-permute-start.8 = (f32[2,256,1]{2,1,0:T(8,128)S(1)}, f32[2,256,1]{2,1,0:T(8,128)S(1)}, u32[]{:S(2)}, u32[]{:S(2)}) collective-permute-start(f32[2,256,1]{2,1,0:T(8,128)S(1)} %get-tuple-element.107), channel_id=1, source_target_pairs={{0,16},{16,32},{32,48},{48,64},{64,80},{80,96},{96,112},{1,17},{17... | collective-permute-start | bytes 6152 | tf_op jit(solution)/shard_map/ppermute | solution.py:25
  101.0 4.5 collective-permute-start.11
  108.8 11.4 %collective-permute-start.13 = (f32[2,256,1]{2,1,0:T(8,128)S(1)}, f32[2,256,1]{2,1,0:T(8,128)S(1)}, u32[]{:S(2)}, u32[]{:S(2)}) collective-permute-start(f32[2,256,1]{2,1,0:T(8,128)S(1)} %get-tuple-element.106), channel_id=1, source_target_pairs={{16,0},{32,16},{48,32},{64,48},{80,64},{96,80},{112,96},{17,1},{33... | collective-permute-start | bytes 6152 | tf_op jit(solution)/shard_map/ppermute | solution.py:27
  110.1 11.7 %collective-permute-start.12 = (f32[2,256,1]{2,1,0:T(8,128)S(1)}, f32[2,256,1]{2,1,0:T(8,128)S(1)}, u32[]{:S(2)}, u32[]{:S(2)}) collective-permute-start(f32[2,256,1]{2,1,0:T(8,128)S(1)} %get-tuple-element.105), channel_id=1, source_target_pairs={{0,16},{16,32},{32,48},{48,64},{64,80},{80,96},{96,112},{1,17},{17... | collective-permute-start | bytes 6152 | tf_op jit(solution)/shard_map/ppermute | solution.py:25
  121.8 4.3 collective-permute-start.15
  128.2 8.4 %collective-permute-start.16 = (f32[256,1]{1,0:T(8,128)S(1)}, f32[256,1]{1,0:T(8,128)S(1)}, u32[]{:S(2)}, u32[]{:S(2)}) collective-permute-start(f32[256,1]{1,0:T(8,128)S(1)} %get-tuple-element.145), channel_id=1, source_target_pairs={{16,0},{32,16},{48,32},{64,48},{80,64},{96,80},{112,96},{17,1},{33... | collective-permute-start | bytes 3080 | tf_op jit(solution)/shard_map/ppermute | solution.py:27
  129.5 8.8 %collective-permute-start.17 = (f32[256,1]{1,0:T(8,128)S(1)}, f32[256,1]{1,0:T(8,128)S(1)}, u32[]{:S(2)}, u32[]{:S(2)}) collective-permute-start(f32[256,1]{1,0:T(8,128)S(1)} %get-tuple-element.144), channel_id=1, source_target_pairs={{0,16},{16,32},{32,48},{48,64},{64,80},{80,96},{96,112},{1,17},{17... | collective-permute-start | bytes 3080 | tf_op jit(solution)/shard_map/ppermute | solution.py:25
  138.8 4.7 collective-permute-start.18
  145.6 10.7 %collective-permute-start.21 = (f32[2,256,1]{2,1,0:T(8,128)S(1)}, f32[2,256,1]{2,1,0:T(8,128)S(1)}, u32[]{:S(2)}, u32[]{:S(2)}) collective-permute-start(f32[2,256,1]{2,1,0:T(8,128)S(1)} %get-tuple-element.104), channel_id=1, source_target_pairs={{16,0},{32,16},{48,32},{64,48},{80,64},{96,80},{112,96},{17,1},{33... | collective-permute-start | bytes 6152 | tf_op jit(solution)/shard_map/ppermute | solution.py:27
  146.9 11.2 %collective-permute-start.20 = (f32[2,256,1]{2,1,0:T(8,128)S(1)}, f32[2,256,1]{2,1,0:T(8,128)S(1)}, u32[]{:S(2)}, u32[]{:S(2)}) collective-permute-start(f32[2,256,1]{2,1,0:T(8,128)S(1)} %get-tuple-element.103), channel_id=1, source_target_pairs={{0,16},{16,32},{32,48},{48,64},{64,80},{80,96},{96,112},{1,17},{17... | collective-permute-start | bytes 6152 | tf_op jit(solution)/shard_map/ppermute | solution.py:25
  158.2 4.4 collective-permute-start.23
  166.1 11.6 %collective-permute-start.25 = (f32[2,256,1]{2,1,0:T(8,128)S(1)}, f32[2,256,1]{2,1,0:T(8,128)S(1)}, u32[]{:S(2)}, u32[]{:S(2)}) collective-permute-start(f32[2,256,1]{2,1,0:T(8,128)S(1)} %get-tuple-element.102), channel_id=1, source_target_pairs={{16,0},{32,16},{48,32},{64,48},{80,64},{96,80},{112,96},{17,1},{33... | collective-permute-start | bytes 6152 | tf_op jit(solution)/shard_map/ppermute | solution.py:27
  167.4 12.1 %collective-permute-start.24 = (f32[2,256,1]{2,1,0:T(8,128)S(1)}, f32[2,256,1]{2,1,0:T(8,128)S(1)}, u32[]{:S(2)}, u32[]{:S(2)}) collective-permute-start(f32[2,256,1]{2,1,0:T(8,128)S(1)} %get-tuple-element.101), channel_id=1, source_target_pairs={{0,16},{16,32},{32,48},{48,64},{64,80},{80,96},{96,112},{1,17},{17... | collective-permute-start | bytes 6152 | tf_op jit(solution)/shard_map/ppermute | solution.py:25
  179.6 4.7 collective-permute-start.27
  186.3 9.4 %collective-permute-start.28 = (f32[256,1]{1,0:T(8,128)S(1)}, f32[256,1]{1,0:T(8,128)S(1)}, u32[]{:S(2)}, u32[]{:S(2)}) collective-permute-start(f32[256,1]{1,0:T(8,128)S(1)} %get-tuple-element.143), channel_id=1, source_target_pairs={{16,0},{32,16},{48,32},{64,48},{80,64},{96,80},{112,96},{17,1},{33... | collective-permute-start | bytes 3080 | tf_op jit(solution)/shard_map/ppermute | solution.py:27
  187.6 9.6 %collective-permute-start.29 = (f32[256,1]{1,0:T(8,128)S(1)}, f32[256,1]{1,0:T(8,128)S(1)}, u32[]{:S(2)}, u32[]{:S(2)}) collective-permute-start(f32[256,1]{1,0:T(8,128)S(1)} %get-tuple-element.142), channel_id=1, source_target_pairs={{0,16},{16,32},{32,48},{48,64},{64,80},{80,96},{96,112},{1,17},{17... | collective-permute-start | bytes 3080 | tf_op jit(solution)/shard_map/ppermute | solution.py:25
  197.7 6.0 collective-permute-start.30
  199.0 4.9 collective-permute-start.31
  205.6 11.2 %collective-permute-start.33 = (f32[2,256,1]{2,1,0:T(8,128)S(1)}, f32[2,256,1]{2,1,0:T(8,128)S(1)}, u32[]{:S(2)}, u32[]{:S(2)}) collective-permute-start(f32[2,256,1]{2,1,0:T(8,128)S(1)} %get-tuple-element.100), channel_id=1, source_target_pairs={{16,0},{32,16},{48,32},{64,48},{80,64},{96,80},{112,96},{17,1},{33... | collective-permute-start | bytes 6152 | tf_op jit(solution)/shard_map/ppermute | solution.py:27
  206.9 11.6 %collective-permute-start.32 = (f32[2,256,1]{2,1,0:T(8,128)S(1)}, f32[2,256,1]{2,1,0:T(8,128)S(1)}, u32[]{:S(2)}, u32[]{:S(2)}) collective-permute-start(f32[2,256,1]{2,1,0:T(8,128)S(1)} %get-tuple-element.99), channel_id=1, source_target_pairs={{0,16},{16,32},{32,48},{48,64},{64,80},{80,96},{96,112},{1,17},{17... | collective-permute-start | bytes 6152 | tf_op jit(solution)/shard_map/ppermute | solution.py:25
  218.6 6.1 collective-permute-start.35
  219.9 5.6 collective-permute-start.34
  228.2 10.8 %collective-permute-start.37 = (f32[2,256,1]{2,1,0:T(8,128)S(1)}, f32[2,256,1]{2,1,0:T(8,128)S(1)}, u32[]{:S(2)}, u32[]{:S(2)}) collective-permute-start(f32[2,256,1]{2,1,0:T(8,128)S(1)} %get-tuple-element.98), channel_id=1, source_target_pairs={{16,0},{32,16},{48,32},{64,48},{80,64},{96,80},{112,96},{17,1},{33... | collective-permute-start | bytes 6152 | tf_op jit(solution)/shard_map/ppermute | solution.py:27
  229.5 11.0 %collective-permute-start.36 = (f32[2,256,1]{2,1,0:T(8,128)S(1)}, f32[2,256,1]{2,1,0:T(8,128)S(1)}, u32[]{:S(2)}, u32[]{:S(2)}) collective-permute-start(f32[2,256,1]{2,1,0:T(8,128)S(1)} %get-tuple-element.97), channel_id=1, source_target_pairs={{0,16},{16,32},{32,48},{48,64},{64,80},{80,96},{96,112},{1,17},{17... | collective-permute-start | bytes 6152 | tf_op jit(solution)/shard_map/ppermute | solution.py:25
  240.6 6.8 collective-permute-start.39
  241.9 6.3 collective-permute-start.38
  249.3 9.4 %collective-permute-start.40 = (f32[256,1]{1,0:T(8,128)S(1)}, f32[256,1]{1,0:T(8,128)S(1)}, u32[]{:S(2)}, u32[]{:S(2)}) collective-permute-start(f32[256,1]{1,0:T(8,128)S(1)} %get-tuple-element.141), channel_id=1, source_target_pairs={{16,0},{32,16},{48,32},{64,48},{80,64},{96,80},{112,96},{17,1},{33... | collective-permute-start | bytes 3080 | tf_op jit(solution)/shard_map/ppermute | solution.py:27
  250.6 9.6 %collective-permute-start.41 = (f32[256,1]{1,0:T(8,128)S(1)}, f32[256,1]{1,0:T(8,128)S(1)}, u32[]{:S(2)}, u32[]{:S(2)}) collective-permute-start(f32[256,1]{1,0:T(8,128)S(1)} %get-tuple-element.140), channel_id=1, source_target_pairs={{0,16},{16,32},{32,48},{48,64},{64,80},{80,96},{96,112},{1,17},{17... | collective-permute-start | bytes 3080 | tf_op jit(solution)/shard_map/ppermute | solution.py:25
  260.8 7.2 %collective-permute-start.42 = (f32[1,258]{1,0:T(1,128)S(1)}, f32[1,258]{1,0:T(1,128)S(1)}, u32[]{:S(2)}, u32[]{:S(2)}) collective-permute-start(f32[1,258]{1,0:T(1,128)S(1)} %get-tuple-element.112), channel_id=1, source_target_pairs={{1,0},{2,1},{3,2},{4,3},{5,4},{6,5},{7,6},{8,7},{9,8},{10,9},{11,1... | collective-permute-start | bytes 3104 | tf_op jit(solution)/shard_map/ppermute | solution.py:27
  262.1 6.0 collective-permute-start.43
  269.7 11.2 %collective-permute-start.45 = (f32[2,256,1]{2,1,0:T(8,128)S(1)}, f32[2,256,1]{2,1,0:T(8,128)S(1)}, u32[]{:S(2)}, u32[]{:S(2)}) collective-permute-start(f32[2,256,1]{2,1,0:T(8,128)S(1)} %get-tuple-element.96), channel_id=1, source_target_pairs={{16,0},{32,16},{48,32},{64,48},{80,64},{96,80},{112,96},{17,1},{33... | collective-permute-start | bytes 6152 | tf_op jit(solution)/shard_map/ppermute | solution.py:27
  271.0 11.7 %collective-permute-start.44 = (f32[2,256,1]{2,1,0:T(8,128)S(1)}, f32[2,256,1]{2,1,0:T(8,128)S(1)}, u32[]{:S(2)}, u32[]{:S(2)}) collective-permute-start(f32[2,256,1]{2,1,0:T(8,128)S(1)} %get-tuple-element.95), channel_id=1, source_target_pairs={{0,16},{16,32},{32,48},{48,64},{64,80},{80,96},{96,112},{1,17},{17... | collective-permute-start | bytes 6152 | tf_op jit(solution)/shard_map/ppermute | solution.py:25
  282.8 6.5 collective-permute-start.47
  284.1 5.6 collective-permute-start.46
  294.1 11.3 %collective-permute-start.49 = (f32[2,256,1]{2,1,0:T(8,128)S(1)}, f32[2,256,1]{2,1,0:T(8,128)S(1)}, u32[]{:S(2)}, u32[]{:S(2)}) collective-permute-start(f32[2,256,1]{2,1,0:T(8,128)S(1)} %get-tuple-element.94), channel_id=1, source_target_pairs={{16,0},{32,16},{48,32},{64,48},{80,64},{96,80},{112,96},{17,1},{33... | collective-permute-start | bytes 6152 | tf_op jit(solution)/shard_map/ppermute | solution.py:27
  295.4 11.7 %collective-permute-start.48 = (f32[2,256,1]{2,1,0:T(8,128)S(1)}, f32[2,256,1]{2,1,0:T(8,128)S(1)}, u32[]{:S(2)}, u32[]{:S(2)}) collective-permute-start(f32[2,256,1]{2,1,0:T(8,128)S(1)} %get-tuple-element.93), channel_id=1, source_target_pairs={{0,16},{16,32},{32,48},{48,64},{64,80},{80,96},{96,112},{1,17},{17... | collective-permute-start | bytes 6152 | tf_op jit(solution)/shard_map/ppermute | solution.py:25
  307.2 6.1 collective-permute-start.51
  308.5 5.6 collective-permute-start.50
  316.6 11.7 %collective-permute-start.53 = (f32[2,256,1]{2,1,0:T(8,128)S(1)}, f32[2,256,1]{2,1,0:T(8,128)S(1)}, u32[]{:S(2)}, u32[]{:S(2)}) collective-permute-start(f32[2,256,1]{2,1,0:T(8,128)S(1)} %get-tuple-element.92), channel_id=1, source_target_pairs={{16,0},{32,16},{48,32},{64,48},{80,64},{96,80},{112,96},{17,1},{33... | collective-permute-start | bytes 6152 | tf_op jit(solution)/shard_map/ppermute | solution.py:27
  317.9 12.1 %collective-permute-start.52 = (f32[2,256,1]{2,1,0:T(8,128)S(1)}, f32[2,256,1]{2,1,0:T(8,128)S(1)}, u32[]{:S(2)}, u32[]{:S(2)}) collective-permute-start(f32[2,256,1]{2,1,0:T(8,128)S(1)} %get-tuple-element.91), channel_id=1, source_target_pairs={{0,16},{16,32},{32,48},{48,64},{64,80},{80,96},{96,112},{1,17},{17... | collective-permute-start | bytes 6152 | tf_op jit(solution)/shard_map/ppermute | solution.py:25
  330.1 5.6 collective-permute-start.55
  331.4 5.1 collective-permute-start.54
  339.0 10.5 %collective-permute-start.57 = (f32[2,256,1]{2,1,0:T(8,128)S(1)}, f32[2,256,1]{2,1,0:T(8,128)S(1)}, u32[]{:S(2)}, u32[]{:S(2)}) collective-permute-start(f32[2,256,1]{2,1,0:T(8,128)S(1)} %get-tuple-element.90), channel_id=1, source_target_pairs={{16,0},{32,16},{48,32},{64,48},{80,64},{96,80},{112,96},{17,1},{33... | collective-permute-start | bytes 6152 | tf_op jit(solution)/shard_map/ppermute | solution.py:27
  340.3 10.7 %collective-permute-start.56 = (f32[2,256,1]{2,1,0:T(8,128)S(1)}, f32[2,256,1]{2,1,0:T(8,128)S(1)}, u32[]{:S(2)}, u32[]{:S(2)}) collective-permute-start(f32[2,256,1]{2,1,0:T(8,128)S(1)} %get-tuple-element.89), channel_id=1, source_target_pairs={{0,16},{16,32},{32,48},{48,64},{64,80},{80,96},{96,112},{1,17},{17... | collective-permute-start | bytes 6152 | tf_op jit(solution)/shard_map/ppermute | solution.py:25
  351.0 7.4 %collective-permute-start.59 = (f32[2,1,258]{2,1,0:T(1,128)S(1)}, f32[2,1,258]{2,1,0:T(1,128)S(1)}, u32[]{:S(2)}, u32[]{:S(2)}) collective-permute-start(f32[2,1,258]{2,1,0:T(1,128)S(1)} %get-tuple-element.37), channel_id=1, source_target_pairs={{1,0},{2,1},{3,2},{4,3},{5,4},{6,5},{7,6},{8,7},{9,8},{10,9},{11,1... | collective-permute-start | bytes 6200 | tf_op jit(solution)/shard_map/ppermute | solution.py:27
  352.3 6.9 collective-permute-start.58
  361.7 10.8 %collective-permute-start.61 = (f32[2,256,1]{2,1,0:T(8,128)S(1)}, f32[2,256,1]{2,1,0:T(8,128)S(1)}, u32[]{:S(2)}, u32[]{:S(2)}) collective-permute-start(f32[2,256,1]{2,1,0:T(8,128)S(1)} %get-tuple-element.88), channel_id=1, source_target_pairs={{16,0},{32,16},{48,32},{64,48},{80,64},{96,80},{112,96},{17,1},{33... | collective-permute-start | bytes 6152 | tf_op jit(solution)/shard_map/ppermute | solution.py:27
  363.0 11.0 %collective-permute-start.60 = (f32[2,256,1]{2,1,0:T(8,128)S(1)}, f32[2,256,1]{2,1,0:T(8,128)S(1)}, u32[]{:S(2)}, u32[]{:S(2)}) collective-permute-start(f32[2,256,1]{2,1,0:T(8,128)S(1)} %get-tuple-element.87), channel_id=1, source_target_pairs={{0,16},{16,32},{32,48},{48,64},{64,80},{80,96},{96,112},{1,17},{17... | collective-permute-start | bytes 6152 | tf_op jit(solution)/shard_map/ppermute | solution.py:25
  374.1 9.8 %collective-permute-start.63 = (f32[2,1,258]{2,1,0:T(1,128)S(1)}, f32[2,1,258]{2,1,0:T(1,128)S(1)}, u32[]{:S(2)}, u32[]{:S(2)}) collective-permute-start(f32[2,1,258]{2,1,0:T(1,128)S(1)} %get-tuple-element.35), channel_id=1, source_target_pairs={{1,0},{2,1},{3,2},{4,3},{5,4},{6,5},{7,6},{8,7},{9,8},{10,9},{11,1... | collective-permute-start | bytes 6200 | tf_op jit(solution)/shard_map/ppermute | solution.py:27
  375.4 9.2 %collective-permute-start.62 = (f32[2,1,258]{2,1,0:T(1,128)S(1)}, f32[2,1,258]{2,1,0:T(1,128)S(1)}, u32[]{:S(2)}, u32[]{:S(2)}) collective-permute-start(f32[2,1,258]{2,1,0:T(1,128)S(1)} %get-tuple-element.36), channel_id=1, source_target_pairs={{0,1},{1,2},{2,3},{3,4},{4,5},{5,6},{6,7},{7,8},{8,9},{9,10},{10,1... | collective-permute-start | bytes 6200 | tf_op jit(solution)/shard_map/ppermute | solution.py:25
  387.0 10.8 %collective-permute-start.65 = (f32[2,256,1]{2,1,0:T(8,128)S(1)}, f32[2,256,1]{2,1,0:T(8,128)S(1)}, u32[]{:S(2)}, u32[]{:S(2)}) collective-permute-start(f32[2,256,1]{2,1,0:T(8,128)S(1)} %get-tuple-element.86), channel_id=1, source_target_pairs={{16,0},{32,16},{48,32},{64,48},{80,64},{96,80},{112,96},{17,1},{33... | collective-permute-start | bytes 6152 | tf_op jit(solution)/shard_map/ppermute | solution.py:27
  388.3 11.0 %collective-permute-start.64 = (f32[2,256,1]{2,1,0:T(8,128)S(1)}, f32[2,256,1]{2,1,0:T(8,128)S(1)}, u32[]{:S(2)}, u32[]{:S(2)}) collective-permute-start(f32[2,256,1]{2,1,0:T(8,128)S(1)} %get-tuple-element.85), channel_id=1, source_target_pairs={{0,16},{16,32},{32,48},{48,64},{64,80},{80,96},{96,112},{1,17},{17... | collective-permute-start | bytes 6152 | tf_op jit(solution)/shard_map/ppermute | solution.py:25
  399.4 9.6 %collective-permute-start.66 = (f32[2,1,258]{2,1,0:T(1,128)S(1)}, f32[2,1,258]{2,1,0:T(1,128)S(1)}, u32[]{:S(2)}, u32[]{:S(2)}) collective-permute-start(f32[2,1,258]{2,1,0:T(1,128)S(1)} %get-tuple-element.34), channel_id=1, source_target_pairs={{0,1},{1,2},{2,3},{3,4},{4,5},{5,6},{6,7},{7,8},{8,9},{9,10},{10,1... | collective-permute-start | bytes 6200 | tf_op jit(solution)/shard_map/ppermute | solution.py:25
  407.1 9.7 %collective-permute-start.67 = (f32[2,1,258]{2,1,0:T(1,128)S(1)}, f32[2,1,258]{2,1,0:T(1,128)S(1)}, u32[]{:S(2)}, u32[]{:S(2)}) collective-permute-start(f32[2,1,258]{2,1,0:T(1,128)S(1)} %get-tuple-element.33), channel_id=1, source_target_pairs={{1,0},{2,1},{3,2},{4,3},{5,4},{6,5},{7,6},{8,7},{9,8},{10,9},{11,1... | collective-permute-start | bytes 6200 | tf_op jit(solution)/shard_map/ppermute | solution.py:27
  434.4 266.7 %all-reduce.4.cloned.1.call-start = ((), (), s32[]{:S(2)}) async-start(), calls=%async_computation | async-start | bytes 131072 | tf_op jit(solution)/shard_map/psum | solution.py:136
  (22 other events, 641.4 us)
Sparse Core Ops, SparseCore 0:
  14.8 49.5 all-gather.2
  434.5 189.2 all-reduce.5
  627.0 74.0 all-reduce.3
where the time goes:
time: 719 us; the launch traced here: 709 us
  waiting for transfers between devices  373 us (52%)
  starting transfers between devices  229 us (32%)
  other arithmetic  48.5 us (7%)
  local copies, waits for them, and re-layouts  37.6 us (5%)
  between operations  16.9 us (2%)
    unnamed x4, waiting for transfers between devices  188 us
    ppermute x34, starting transfers between devices, with_halo(): lax.ppermute(tail, axis, [(i, (i + 1) % count) for i in range(ends)])  185 us
    psum x1, waiting for transfers between devices, per_device(): gradient = lax.psum(partial_sum, 'gx')  75.7 us
    ppermute x34, waiting for transfers between devices, with_halo(): lax.ppermute(head, axis, [((i + 1) % count, i) for i in range(ends)])  53.8 us
    ppermute x34, starting transfers between devices, with_halo(): lax.ppermute(head, axis, [((i + 1) % count, i) for i in range(ends)])  43.9 us
    ppermute x34, waiting for transfers between devices, with_halo(): lax.ppermute(tail, axis, [(i, (i + 1) % count) for i in range(ends)])  35.8 us
    all_gather x1, waiting for transfers between devices, per_device(): shard_rows = lax.all_gather(rates, 'gy', axis=0, tiled=True)  19.9 us
    another operation x36, other arithmetic, relaxation(): return jnp.stack([new_u, new_v])  15.8 us
  transfers between devices with their start and end apart: 71, of which 52 were waited for; matrix products, arithmetic and copies ran while one was open for 2% of the time, Pallas kernels for 0%

commit v1 on v0

--- a/solution.py
+++ b/solution.py
@@ -133,7 +133,7 @@
         scatter_dimension=0,
         tiled=True,
     )
-    gradient = lax.psum(partial_sum, "gx")
+    gradient = jnp.sum(lax.all_gather(partial_sum, "gx"), axis=0)
     return (velocity[0], velocity[1], gradient)
 
 

time: 719 us -> 671 us (0.933)
  waiting for transfers between devices: 373 us -> 299 us
  blocking collectives: 0 us -> 29 us
    psum x1 -> x0, waiting for transfers between devices: 75.7 us -> none  [per_device(): gradient = lax.psum(partial_sum, 'gx')]
    all_gather x0 -> x1, blocking collectives: none -> 29 us  [per_device(): gradient = jnp.sum(lax.all_gather(partial_sum, 'gx'), axis=0)]
    unnamed x4 -> x3, waiting for transfers between devices: 188 us -> 188 us
  transfers between devices with their start and end apart: 71 -> 70, of which waited for: 52 -> 51; matrix products, arithmetic and copies ran while one was open for 2% -> 2% of each run, Pallas kernels for 0% -> 0%
where the time goes in v1:
time: 671 us; the launch traced here: 661 us
  waiting for transfers between devices  299 us (45%)
  starting transfers between devices  229 us (34%)
  other arithmetic  49.1 us (7%)
  local copies, waits for them, and re-layouts  34.7 us (5%)
  blocking collectives  29 us (4%)
  between operations  17.2 us (3%)
    unnamed x3, waiting for transfers between devices  188 us
    ppermute x34, starting transfers between devices, with_halo(): lax.ppermute(tail, axis, [(i, (i + 1) % count) for i in range(ends)])  185 us
    ppermute x34, waiting for transfers between devices, with_halo(): lax.ppermute(head, axis, [((i + 1) % count, i) for i in range(ends)])  53.8 us
    ppermute x34, starting transfers between devices, with_halo(): lax.ppermute(head, axis, [((i + 1) % count, i) for i in range(ends)])  43.9 us
    ppermute x34, waiting for transfers between devices, with_halo(): lax.ppermute(tail, axis, [(i, (i + 1) % count) for i in range(ends)])  35.9 us
    all_gather x1, blocking collectives, per_device(): gradient = jnp.sum(lax.all_gather(partial_sum, 'gx'), axis=0)  29 us
    all_gather x1, waiting for transfers between devices, per_device(): shard_rows = lax.all_gather(rates, 'gy', axis=0, tiled=True)  20.7 us
    another operation x36, other arithmetic, relaxation(): return jnp.stack([new_u, new_v])  15.8 us
  transfers between devices with their start and end apart: 70, of which 51 were waited for; matrix products, arithmetic and copies ran while one was open for 2% of the time, Pallas kernels for 0%

profile of v1, /device:TPU:0, one launch (start us, length us, event | category | flops | bytes accessed | tf_op | source)
XLA Modules:
  0.0 661.4 jit_solution(17884321620362670657)
XLA Ops:
  8.6 4.6 collective-permute-start
  14.7 2.8 collective-permute-done.1
  20.1 3.0 collective-permute-start.2
  26.5 5.0 collective-permute-start.5
  37.8 3.0 collective-permute-start.7
  43.7 20.7 %all-gather.5.cloned.1.call-done = f32[16,4,4096]{2,1,0:T(4,128)} async-done(((f32[1,4,4096]{2,1,0:T(4,128)}), f32[16,4,4096]{2,1,0:T(4,128)}) %all-gather.5.cloned.1.call-update) | async-done | bytes 1048592 | tf_op jit(solution)/shard_map/all_gather | solution.py:100
  64.3 2.6 reshape.218
  66.9 3.1 reshape.211
  70.0 4.0 fusion
  74.0 4.0 broadcast_in_dim.7
  78.0 8.4 %broadcast_in_dim.8 = f32[256,256]{1,0:T(8,128)S(1)} reshape(f32[64,4,64,4]{3,2,1,0:T(8,128)} %broadcast_in_dim.7) | data formatting | bytes 524288 | tf_op jit(solution)/shard_map/broadcast_in_dim | solution.py:104
  86.3 2.1 fusion.435
  90.5 4.7 collective-permute-start.8
  95.2 4.4 collective-permute-done.9
  102.2 3.2 collective-permute-start.10
  110.0 5.2 collective-permute-start.12
  115.2 5.0 collective-permute-done.13
  123.1 3.0 collective-permute-start.14
  129.5 5.0 collective-permute-start.17
  134.5 2.1 collective-permute-done.16
  140.0 3.0 collective-permute-start.19
  146.8 5.0 collective-permute-start.20
  151.9 4.4 collective-permute-done.21
  156.3 1.8 collective-permute-done.20
  159.5 3.1 collective-permute-start.22
  167.3 6.2 collective-permute-start.24
  173.5 4.2 collective-permute-done.25
  177.7 1.8 collective-permute-done.24
  180.8 3.4 collective-permute-start.26
  187.5 7.1 %collective-permute-start.29 = (f32[256,1]{1,0:T(8,128)S(1)}, f32[256,1]{1,0:T(8,128)S(1)}, u32[]{:S(2)}, u32[]{:S(2)}) collective-permute-start(f32[256,1]{1,0:T(8,128)S(1)} %get-tuple-element.142), channel_id=1, source_target_pairs={{0,16},{16,32},{32,48},{48,64},{64,80},{80,96},{96,112},{1,17},{17... | collective-permute-start | bytes 3080 | tf_op jit(solution)/shard_map/ppermute | solution.py:25
  199.0 4.3 collective-permute-start.31
  206.9 7.1 %collective-permute-start.32 = (f32[2,256,1]{2,1,0:T(8,128)S(1)}, f32[2,256,1]{2,1,0:T(8,128)S(1)}, u32[]{:S(2)}, u32[]{:S(2)}) collective-permute-start(f32[2,256,1]{2,1,0:T(8,128)S(1)} %get-tuple-element.99), channel_id=1, source_target_pairs={{0,16},{16,32},{32,48},{48,64},{64,80},{80,96},{96,112},{1,17},{17... | collective-permute-start | bytes 6152 | tf_op jit(solution)/shard_map/ppermute | solution.py:25
  214.0 2.8 collective-permute-done.33
  216.8 1.7 collective-permute-done.32
  219.9 4.8 collective-permute-start.34
  229.4 7.1 %collective-permute-start.36 = (f32[2,256,1]{2,1,0:T(8,128)S(1)}, f32[2,256,1]{2,1,0:T(8,128)S(1)}, u32[]{:S(2)}, u32[]{:S(2)}) collective-permute-start(f32[2,256,1]{2,1,0:T(8,128)S(1)} %get-tuple-element.97), channel_id=1, source_target_pairs={{0,16},{16,32},{32,48},{48,64},{64,80},{80,96},{96,112},{1,17},{17... | collective-permute-start | bytes 6152 | tf_op jit(solution)/shard_map/ppermute | solution.py:25
  236.6 2.4 collective-permute-done.37
  241.8 5.5 collective-permute-start.38
  250.6 7.1 %collective-permute-start.41 = (f32[256,1]{1,0:T(8,128)S(1)}, f32[256,1]{1,0:T(8,128)S(1)}, u32[]{:S(2)}, u32[]{:S(2)}) collective-permute-start(f32[256,1]{1,0:T(8,128)S(1)} %get-tuple-element.140), channel_id=1, source_target_pairs={{0,16},{16,32},{32,48},{48,64},{64,80},{80,96},{96,112},{1,17},{17... | collective-permute-start | bytes 3080 | tf_op jit(solution)/shard_map/ppermute | solution.py:25
  262.0 5.2 collective-permute-start.43
  271.0 7.1 %collective-permute-start.44 = (f32[2,256,1]{2,1,0:T(8,128)S(1)}, f32[2,256,1]{2,1,0:T(8,128)S(1)}, u32[]{:S(2)}, u32[]{:S(2)}) collective-permute-start(f32[2,256,1]{2,1,0:T(8,128)S(1)} %get-tuple-element.95), channel_id=1, source_target_pairs={{0,16},{16,32},{32,48},{48,64},{64,80},{80,96},{96,112},{1,17},{17... | collective-permute-start | bytes 6152 | tf_op jit(solution)/shard_map/ppermute | solution.py:25
  278.1 2.8 collective-permute-done.45
  284.0 5.2 collective-permute-start.46
  295.4 7.1 %collective-permute-start.48 = (f32[2,256,1]{2,1,0:T(8,128)S(1)}, f32[2,256,1]{2,1,0:T(8,128)S(1)}, u32[]{:S(2)}, u32[]{:S(2)}) collective-permute-start(f32[2,256,1]{2,1,0:T(8,128)S(1)} %get-tuple-element.93), channel_id=1, source_target_pairs={{0,16},{16,32},{32,48},{48,64},{64,80},{80,96},{96,112},{1,17},{17... | collective-permute-start | bytes 6152 | tf_op jit(solution)/shard_map/ppermute | solution.py:25
  302.5 2.8 collective-permute-done.49
  305.3 1.7 collective-permute-done.48
  308.5 4.8 collective-permute-start.50
  317.8 7.1 %collective-permute-start.52 = (f32[2,256,1]{2,1,0:T(8,128)S(1)}, f32[2,256,1]{2,1,0:T(8,128)S(1)}, u32[]{:S(2)}, u32[]{:S(2)}) collective-permute-start(f32[2,256,1]{2,1,0:T(8,128)S(1)} %get-tuple-element.91), channel_id=1, source_target_pairs={{0,16},{16,32},{32,48},{48,64},{64,80},{80,96},{96,112},{1,17},{17... | collective-permute-start | bytes 6152 | tf_op jit(solution)/shard_map/ppermute | solution.py:25
  324.9 3.2 collective-permute-done.53
  331.3 4.3 collective-permute-start.54
  340.2 6.8 %collective-permute-start.56 = (f32[2,256,1]{2,1,0:T(8,128)S(1)}, f32[2,256,1]{2,1,0:T(8,128)S(1)}, u32[]{:S(2)}, u32[]{:S(2)}) collective-permute-start(f32[2,256,1]{2,1,0:T(8,128)S(1)} %get-tuple-element.89), channel_id=1, source_target_pairs={{0,16},{16,32},{32,48},{48,64},{64,80},{80,96},{96,112},{1,17},{17... | collective-permute-start | bytes 6152 | tf_op jit(solution)/shard_map/ppermute | solution.py:25
  347.0 2.4 collective-permute-done.57
  352.3 6.1 collective-permute-start.58
  363.0 7.1 %collective-permute-start.60 = (f32[2,256,1]{2,1,0:T(8,128)S(1)}, f32[2,256,1]{2,1,0:T(8,128)S(1)}, u32[]{:S(2)}, u32[]{:S(2)}) collective-permute-start(f32[2,256,1]{2,1,0:T(8,128)S(1)} %get-tuple-element.87), channel_id=1, source_target_pairs={{0,16},{16,32},{32,48},{48,64},{64,80},{80,96},{96,112},{1,17},{17... | collective-permute-start | bytes 6152 | tf_op jit(solution)/shard_map/ppermute | solution.py:25
  370.1 2.4 collective-permute-done.61
  375.4 8.5 %collective-permute-start.62 = (f32[2,1,258]{2,1,0:T(1,128)S(1)}, f32[2,1,258]{2,1,0:T(1,128)S(1)}, u32[]{:S(2)}, u32[]{:S(2)}) collective-permute-start(f32[2,1,258]{2,1,0:T(1,128)S(1)} %get-tuple-element.36), channel_id=1, source_target_pairs={{0,1},{1,2},{2,3},{3,4},{4,5},{5,6},{6,7},{7,8},{8,9},{9,10},{10,1... | collective-permute-start | bytes 6200 | tf_op jit(solution)/shard_map/ppermute | solution.py:25
  388.3 7.1 %collective-permute-start.64 = (f32[2,256,1]{2,1,0:T(8,128)S(1)}, f32[2,256,1]{2,1,0:T(8,128)S(1)}, u32[]{:S(2)}, u32[]{:S(2)}) collective-permute-start(f32[2,256,1]{2,1,0:T(8,128)S(1)} %get-tuple-element.85), channel_id=1, source_target_pairs={{0,16},{16,32},{32,48},{48,64},{64,80},{80,96},{96,112},{1,17},{17... | collective-permute-start | bytes 6152 | tf_op jit(solution)/shard_map/ppermute | solution.py:25
  395.4 2.4 collective-permute-done.65
  399.4 7.7 %collective-permute-start.66 = (f32[2,1,258]{2,1,0:T(1,128)S(1)}, f32[2,1,258]{2,1,0:T(1,128)S(1)}, u32[]{:S(2)}, u32[]{:S(2)}) collective-permute-start(f32[2,1,258]{2,1,0:T(1,128)S(1)} %get-tuple-element.34), channel_id=1, source_target_pairs={{0,1},{1,2},{2,3},{3,4},{4,5},{5,6},{6,7},{7,8},{8,9},{9,10},{10,1... | collective-permute-start | bytes 6200 | tf_op jit(solution)/shard_map/ppermute | solution.py:25
  409.0 7.8 %collective-permute-done.67 = f32[2,1,258]{2,1,0:T(1,128)S(1)} collective-permute-done((f32[2,1,258]{2,1,0:T(1,128)S(1)}, f32[2,1,258]{2,1,0:T(1,128)S(1)}, u32[]{:S(2)}, u32[]{:S(2)}) %collective-permute-start.67) | collective-permute-done | bytes 2096 | tf_op jit(solution)/shard_map/ppermute | solution.py:27
  419.0 10.1 %reshape.213 = f32[64,4,64,4]{3,2,1,0:T(8,128)} reshape(f32[256,256]{1,0:T(8,128)S(1)} %fusion.161) | data formatting | bytes 524288 | tf_op jit(solution)/shard_map/reshape | solution.py:126
  429.1 4.1 reduce_sum.18
  435.6 188.2 %all-reduce.3.cloned.1.call-done = f32[64,4096]{1,0:T(8,128)} async-done(((f32[64,4096]{1,0:T(8,128)}), f32[64,4096]{1,0:T(8,128)}) %all-reduce.3.cloned.1.call-update) | async-done | bytes 1048592
  624.7 29.0 %all-gather.2 = f32[8,4,4096]{2,1,0:T(4,128)S(1)} all-gather(f32[1,4,4096]{2,1,0:T(4,128)S(1)} %dynamic-slice_bitcast_fusion), channel_id=2, replica_groups=mesh['gx'=8,'gy'=16] {'gx'}, dimensions={0}, use_global_device_ids=true | all-gather | bytes 589824 | tf_op jit(solution)/shard_map/all_gather | solution.py:136
  (262 shorter events, 124.6 us)
Async XLA Ops:
  7.2 57.2 %all-gather.5.cloned.1.call-start = ((), (), s32[]{:S(2)}) async-start(), calls=%async_computation | async-start | bytes 1114112 | tf_op jit(solution)/shard_map/all_gather | solution.py:100
  7.3 10.2 %collective-permute-start.1 = (f32[2,256,1]{2,1,0:T(8,128)S(1)}, f32[2,256,1]{2,1,0:T(8,128)S(1)}, u32[]{:S(2)}, u32[]{:S(2)}) collective-permute-start(f32[2,256,1]{2,1,0:T(8,128)S(1)} %broadcast.112), channel_id=1, source_target_pairs={{16,0},{32,16},{48,32},{64,48},{80,64},{96,80},{112,96},{17,1},{33... | collective-permute-start | bytes 6152 | tf_op jit(solution)/shard_map/ppermute | solution.py:27
  8.6 10.1 %collective-permute-start = (f32[2,256,1]{2,1,0:T(8,128)S(1)}, f32[2,256,1]{2,1,0:T(8,128)S(1)}, u32[]{:S(2)}, u32[]{:S(2)}) collective-permute-start(f32[2,256,1]{2,1,0:T(8,128)S(1)} %broadcast.112), channel_id=1, source_target_pairs={{0,16},{16,32},{32,48},{48,64},{64,80},{80,96},{96,112},{1,17},{17... | collective-permute-start | bytes 6152 | tf_op jit(solution)/shard_map/ppermute | solution.py:25
  14.6 609.1 %all-reduce.3.cloned.1.call-start = ((), (), s32[]{:S(2)}) async-start(), calls=%async_computation.1 | async-start | bytes 2097152
  18.8 4.3 collective-permute-start.3
  25.2 8.8 %collective-permute-start.4 = (f32[256,1]{1,0:T(8,128)S(1)}, f32[256,1]{1,0:T(8,128)S(1)}, u32[]{:S(2)}, u32[]{:S(2)}) collective-permute-start(f32[256,1]{1,0:T(8,128)S(1)} %get-tuple-element.147), channel_id=1, source_target_pairs={{16,0},{32,16},{48,32},{64,48},{80,64},{96,80},{112,96},{17,1},{33... | collective-permute-start | bytes 3080 | tf_op jit(solution)/shard_map/ppermute | solution.py:27
  26.5 8.8 %collective-permute-start.5 = (f32[256,1]{1,0:T(8,128)S(1)}, f32[256,1]{1,0:T(8,128)S(1)}, u32[]{:S(2)}, u32[]{:S(2)}) collective-permute-start(f32[256,1]{1,0:T(8,128)S(1)} %get-tuple-element.146), channel_id=1, source_target_pairs={{0,16},{16,32},{32,48},{48,64},{64,80},{80,96},{96,112},{1,17},{17... | collective-permute-start | bytes 3080 | tf_op jit(solution)/shard_map/ppermute | solution.py:25
  36.5 5.4 collective-permute-start.6
  89.2 10.4 %collective-permute-start.9 = (f32[2,256,1]{2,1,0:T(8,128)S(1)}, f32[2,256,1]{2,1,0:T(8,128)S(1)}, u32[]{:S(2)}, u32[]{:S(2)}) collective-permute-start(f32[2,256,1]{2,1,0:T(8,128)S(1)} %get-tuple-element.108), channel_id=1, source_target_pairs={{16,0},{32,16},{48,32},{64,48},{80,64},{96,80},{112,96},{17,1},{33... | collective-permute-start | bytes 6152 | tf_op jit(solution)/shard_map/ppermute | solution.py:27
  90.5 10.4 %collective-permute-start.8 = (f32[2,256,1]{2,1,0:T(8,128)S(1)}, f32[2,256,1]{2,1,0:T(8,128)S(1)}, u32[]{:S(2)}, u32[]{:S(2)}) collective-permute-start(f32[2,256,1]{2,1,0:T(8,128)S(1)} %get-tuple-element.107), channel_id=1, source_target_pairs={{0,16},{16,32},{32,48},{48,64},{64,80},{80,96},{96,112},{1,17},{17... | collective-permute-start | bytes 6152 | tf_op jit(solution)/shard_map/ppermute | solution.py:25
  100.9 4.5 collective-permute-start.11
  108.7 11.4 %collective-permute-start.13 = (f32[2,256,1]{2,1,0:T(8,128)S(1)}, f32[2,256,1]{2,1,0:T(8,128)S(1)}, u32[]{:S(2)}, u32[]{:S(2)}) collective-permute-start(f32[2,256,1]{2,1,0:T(8,128)S(1)} %get-tuple-element.106), channel_id=1, source_target_pairs={{16,0},{32,16},{48,32},{64,48},{80,64},{96,80},{112,96},{17,1},{33... | collective-permute-start | bytes 6152 | tf_op jit(solution)/shard_map/ppermute | solution.py:27
  110.0 11.7 %collective-permute-start.12 = (f32[2,256,1]{2,1,0:T(8,128)S(1)}, f32[2,256,1]{2,1,0:T(8,128)S(1)}, u32[]{:S(2)}, u32[]{:S(2)}) collective-permute-start(f32[2,256,1]{2,1,0:T(8,128)S(1)} %get-tuple-element.105), channel_id=1, source_target_pairs={{0,16},{16,32},{32,48},{48,64},{64,80},{80,96},{96,112},{1,17},{17... | collective-permute-start | bytes 6152 | tf_op jit(solution)/shard_map/ppermute | solution.py:25
  121.8 4.3 collective-permute-start.15
  128.2 8.4 %collective-permute-start.16 = (f32[256,1]{1,0:T(8,128)S(1)}, f32[256,1]{1,0:T(8,128)S(1)}, u32[]{:S(2)}, u32[]{:S(2)}) collective-permute-start(f32[256,1]{1,0:T(8,128)S(1)} %get-tuple-element.145), channel_id=1, source_target_pairs={{16,0},{32,16},{48,32},{64,48},{80,64},{96,80},{112,96},{17,1},{33... | collective-permute-start | bytes 3080 | tf_op jit(solution)/shard_map/ppermute | solution.py:27
  129.5 8.8 %collective-permute-start.17 = (f32[256,1]{1,0:T(8,128)S(1)}, f32[256,1]{1,0:T(8,128)S(1)}, u32[]{:S(2)}, u32[]{:S(2)}) collective-permute-start(f32[256,1]{1,0:T(8,128)S(1)} %get-tuple-element.144), channel_id=1, source_target_pairs={{0,16},{16,32},{32,48},{48,64},{64,80},{80,96},{96,112},{1,17},{17... | collective-permute-start | bytes 3080 | tf_op jit(solution)/shard_map/ppermute | solution.py:25
  138.7 4.7 collective-permute-start.18
  145.5 10.7 %collective-permute-start.21 = (f32[2,256,1]{2,1,0:T(8,128)S(1)}, f32[2,256,1]{2,1,0:T(8,128)S(1)}, u32[]{:S(2)}, u32[]{:S(2)}) collective-permute-start(f32[2,256,1]{2,1,0:T(8,128)S(1)} %get-tuple-element.104), channel_id=1, source_target_pairs={{16,0},{32,16},{48,32},{64,48},{80,64},{96,80},{112,96},{17,1},{33... | collective-permute-start | bytes 6152 | tf_op jit(solution)/shard_map/ppermute | solution.py:27
  146.8 11.2 %collective-permute-start.20 = (f32[2,256,1]{2,1,0:T(8,128)S(1)}, f32[2,256,1]{2,1,0:T(8,128)S(1)}, u32[]{:S(2)}, u32[]{:S(2)}) collective-permute-start(f32[2,256,1]{2,1,0:T(8,128)S(1)} %get-tuple-element.103), channel_id=1, source_target_pairs={{0,16},{16,32},{32,48},{48,64},{64,80},{80,96},{96,112},{1,17},{17... | collective-permute-start | bytes 6152 | tf_op jit(solution)/shard_map/ppermute | solution.py:25
  158.2 4.4 collective-permute-start.23
  166.0 11.6 %collective-permute-start.25 = (f32[2,256,1]{2,1,0:T(8,128)S(1)}, f32[2,256,1]{2,1,0:T(8,128)S(1)}, u32[]{:S(2)}, u32[]{:S(2)}) collective-permute-start(f32[2,256,1]{2,1,0:T(8,128)S(1)} %get-tuple-element.102), channel_id=1, source_target_pairs={{16,0},{32,16},{48,32},{64,48},{80,64},{96,80},{112,96},{17,1},{33... | collective-permute-start | bytes 6152 | tf_op jit(solution)/shard_map/ppermute | solution.py:27
  167.3 12.1 %collective-permute-start.24 = (f32[2,256,1]{2,1,0:T(8,128)S(1)}, f32[2,256,1]{2,1,0:T(8,128)S(1)}, u32[]{:S(2)}, u32[]{:S(2)}) collective-permute-start(f32[2,256,1]{2,1,0:T(8,128)S(1)} %get-tuple-element.101), channel_id=1, source_target_pairs={{0,16},{16,32},{32,48},{48,64},{64,80},{80,96},{96,112},{1,17},{17... | collective-permute-start | bytes 6152 | tf_op jit(solution)/shard_map/ppermute | solution.py:25
  179.5 4.7 collective-permute-start.27
  180.8 4.2 collective-permute-start.26
  186.2 9.4 %collective-permute-start.28 = (f32[256,1]{1,0:T(8,128)S(1)}, f32[256,1]{1,0:T(8,128)S(1)}, u32[]{:S(2)}, u32[]{:S(2)}) collective-permute-start(f32[256,1]{1,0:T(8,128)S(1)} %get-tuple-element.143), channel_id=1, source_target_pairs={{16,0},{32,16},{48,32},{64,48},{80,64},{96,80},{112,96},{17,1},{33... | collective-permute-start | bytes 3080 | tf_op jit(solution)/shard_map/ppermute | solution.py:27
  187.5 9.6 %collective-permute-start.29 = (f32[256,1]{1,0:T(8,128)S(1)}, f32[256,1]{1,0:T(8,128)S(1)}, u32[]{:S(2)}, u32[]{:S(2)}) collective-permute-start(f32[256,1]{1,0:T(8,128)S(1)} %get-tuple-element.142), channel_id=1, source_target_pairs={{0,16},{16,32},{32,48},{48,64},{64,80},{80,96},{96,112},{1,17},{17... | collective-permute-start | bytes 3080 | tf_op jit(solution)/shard_map/ppermute | solution.py:25
  197.7 6.0 collective-permute-start.30
  199.0 4.9 collective-permute-start.31
  205.6 11.2 %collective-permute-start.33 = (f32[2,256,1]{2,1,0:T(8,128)S(1)}, f32[2,256,1]{2,1,0:T(8,128)S(1)}, u32[]{:S(2)}, u32[]{:S(2)}) collective-permute-start(f32[2,256,1]{2,1,0:T(8,128)S(1)} %get-tuple-element.100), channel_id=1, source_target_pairs={{16,0},{32,16},{48,32},{64,48},{80,64},{96,80},{112,96},{17,1},{33... | collective-permute-start | bytes 6152 | tf_op jit(solution)/shard_map/ppermute | solution.py:27
  206.9 11.6 %collective-permute-start.32 = (f32[2,256,1]{2,1,0:T(8,128)S(1)}, f32[2,256,1]{2,1,0:T(8,128)S(1)}, u32[]{:S(2)}, u32[]{:S(2)}) collective-permute-start(f32[2,256,1]{2,1,0:T(8,128)S(1)} %get-tuple-element.99), channel_id=1, source_target_pairs={{0,16},{16,32},{32,48},{48,64},{64,80},{80,96},{96,112},{1,17},{17... | collective-permute-start | bytes 6152 | tf_op jit(solution)/shard_map/ppermute | solution.py:25
  218.6 6.1 collective-permute-start.35
  219.9 5.6 collective-permute-start.34
  228.1 10.8 %collective-permute-start.37 = (f32[2,256,1]{2,1,0:T(8,128)S(1)}, f32[2,256,1]{2,1,0:T(8,128)S(1)}, u32[]{:S(2)}, u32[]{:S(2)}) collective-permute-start(f32[2,256,1]{2,1,0:T(8,128)S(1)} %get-tuple-element.98), channel_id=1, source_target_pairs={{16,0},{32,16},{48,32},{64,48},{80,64},{96,80},{112,96},{17,1},{33... | collective-permute-start | bytes 6152 | tf_op jit(solution)/shard_map/ppermute | solution.py:27
  229.4 11.0 %collective-permute-start.36 = (f32[2,256,1]{2,1,0:T(8,128)S(1)}, f32[2,256,1]{2,1,0:T(8,128)S(1)}, u32[]{:S(2)}, u32[]{:S(2)}) collective-permute-start(f32[2,256,1]{2,1,0:T(8,128)S(1)} %get-tuple-element.97), channel_id=1, source_target_pairs={{0,16},{16,32},{32,48},{48,64},{64,80},{80,96},{96,112},{1,17},{17... | collective-permute-start | bytes 6152 | tf_op jit(solution)/shard_map/ppermute | solution.py:25
  240.5 6.8 %collective-permute-start.39 = (f32[2,1,258]{2,1,0:T(1,128)S(1)}, f32[2,1,258]{2,1,0:T(1,128)S(1)}, u32[]{:S(2)}, u32[]{:S(2)}) collective-permute-start(f32[2,1,258]{2,1,0:T(1,128)S(1)} %get-tuple-element.46), channel_id=1, source_target_pairs={{1,0},{2,1},{3,2},{4,3},{5,4},{6,5},{7,6},{8,7},{9,8},{10,9},{11,1... | collective-permute-start | bytes 6200 | tf_op jit(solution)/shard_map/ppermute | solution.py:27
  241.8 6.3 collective-permute-start.38
  249.3 9.4 %collective-permute-start.40 = (f32[256,1]{1,0:T(8,128)S(1)}, f32[256,1]{1,0:T(8,128)S(1)}, u32[]{:S(2)}, u32[]{:S(2)}) collective-permute-start(f32[256,1]{1,0:T(8,128)S(1)} %get-tuple-element.141), channel_id=1, source_target_pairs={{16,0},{32,16},{48,32},{64,48},{80,64},{96,80},{112,96},{17,1},{33... | collective-permute-start | bytes 3080 | tf_op jit(solution)/shard_map/ppermute | solution.py:27
  250.6 9.6 %collective-permute-start.41 = (f32[256,1]{1,0:T(8,128)S(1)}, f32[256,1]{1,0:T(8,128)S(1)}, u32[]{:S(2)}, u32[]{:S(2)}) collective-permute-start(f32[256,1]{1,0:T(8,128)S(1)} %get-tuple-element.140), channel_id=1, source_target_pairs={{0,16},{16,32},{32,48},{48,64},{64,80},{80,96},{96,112},{1,17},{17... | collective-permute-start | bytes 3080 | tf_op jit(solution)/shard_map/ppermute | solution.py:25
  260.7 7.2 %collective-permute-start.42 = (f32[1,258]{1,0:T(1,128)S(1)}, f32[1,258]{1,0:T(1,128)S(1)}, u32[]{:S(2)}, u32[]{:S(2)}) collective-permute-start(f32[1,258]{1,0:T(1,128)S(1)} %get-tuple-element.112), channel_id=1, source_target_pairs={{1,0},{2,1},{3,2},{4,3},{5,4},{6,5},{7,6},{8,7},{9,8},{10,9},{11,1... | collective-permute-start | bytes 3104 | tf_op jit(solution)/shard_map/ppermute | solution.py:27
  262.0 6.0 collective-permute-start.43
  269.7 11.2 %collective-permute-start.45 = (f32[2,256,1]{2,1,0:T(8,128)S(1)}, f32[2,256,1]{2,1,0:T(8,128)S(1)}, u32[]{:S(2)}, u32[]{:S(2)}) collective-permute-start(f32[2,256,1]{2,1,0:T(8,128)S(1)} %get-tuple-element.96), channel_id=1, source_target_pairs={{16,0},{32,16},{48,32},{64,48},{80,64},{96,80},{112,96},{17,1},{33... | collective-permute-start | bytes 6152 | tf_op jit(solution)/shard_map/ppermute | solution.py:27
  271.0 11.7 %collective-permute-start.44 = (f32[2,256,1]{2,1,0:T(8,128)S(1)}, f32[2,256,1]{2,1,0:T(8,128)S(1)}, u32[]{:S(2)}, u32[]{:S(2)}) collective-permute-start(f32[2,256,1]{2,1,0:T(8,128)S(1)} %get-tuple-element.95), channel_id=1, source_target_pairs={{0,16},{16,32},{32,48},{48,64},{64,80},{80,96},{96,112},{1,17},{17... | collective-permute-start | bytes 6152 | tf_op jit(solution)/shard_map/ppermute | solution.py:25
  282.7 6.5 collective-permute-start.47
  284.0 5.6 collective-permute-start.46
  294.1 11.3 %collective-permute-start.49 = (f32[2,256,1]{2,1,0:T(8,128)S(1)}, f32[2,256,1]{2,1,0:T(8,128)S(1)}, u32[]{:S(2)}, u32[]{:S(2)}) collective-permute-start(f32[2,256,1]{2,1,0:T(8,128)S(1)} %get-tuple-element.94), channel_id=1, source_target_pairs={{16,0},{32,16},{48,32},{64,48},{80,64},{96,80},{112,96},{17,1},{33... | collective-permute-start | bytes 6152 | tf_op jit(solution)/shard_map/ppermute | solution.py:27
  295.4 11.7 %collective-permute-start.48 = (f32[2,256,1]{2,1,0:T(8,128)S(1)}, f32[2,256,1]{2,1,0:T(8,128)S(1)}, u32[]{:S(2)}, u32[]{:S(2)}) collective-permute-start(f32[2,256,1]{2,1,0:T(8,128)S(1)} %get-tuple-element.93), channel_id=1, source_target_pairs={{0,16},{16,32},{32,48},{48,64},{64,80},{80,96},{96,112},{1,17},{17... | collective-permute-start | bytes 6152 | tf_op jit(solution)/shard_map/ppermute | solution.py:25
  307.2 6.1 collective-permute-start.51
  308.5 5.6 collective-permute-start.50
  316.5 11.7 %collective-permute-start.53 = (f32[2,256,1]{2,1,0:T(8,128)S(1)}, f32[2,256,1]{2,1,0:T(8,128)S(1)}, u32[]{:S(2)}, u32[]{:S(2)}) collective-permute-start(f32[2,256,1]{2,1,0:T(8,128)S(1)} %get-tuple-element.92), channel_id=1, source_target_pairs={{16,0},{32,16},{48,32},{64,48},{80,64},{96,80},{112,96},{17,1},{33... | collective-permute-start | bytes 6152 | tf_op jit(solution)/shard_map/ppermute | solution.py:27
  317.8 12.1 %collective-permute-start.52 = (f32[2,256,1]{2,1,0:T(8,128)S(1)}, f32[2,256,1]{2,1,0:T(8,128)S(1)}, u32[]{:S(2)}, u32[]{:S(2)}) collective-permute-start(f32[2,256,1]{2,1,0:T(8,128)S(1)} %get-tuple-element.91), channel_id=1, source_target_pairs={{0,16},{16,32},{32,48},{48,64},{64,80},{80,96},{96,112},{1,17},{17... | collective-permute-start | bytes 6152 | tf_op jit(solution)/shard_map/ppermute | solution.py:25
  330.0 5.6 collective-permute-start.55
  331.3 5.1 collective-permute-start.54
  338.9 10.5 %collective-permute-start.57 = (f32[2,256,1]{2,1,0:T(8,128)S(1)}, f32[2,256,1]{2,1,0:T(8,128)S(1)}, u32[]{:S(2)}, u32[]{:S(2)}) collective-permute-start(f32[2,256,1]{2,1,0:T(8,128)S(1)} %get-tuple-element.90), channel_id=1, source_target_pairs={{16,0},{32,16},{48,32},{64,48},{80,64},{96,80},{112,96},{17,1},{33... | collective-permute-start | bytes 6152 | tf_op jit(solution)/shard_map/ppermute | solution.py:27
  340.2 10.7 %collective-permute-start.56 = (f32[2,256,1]{2,1,0:T(8,128)S(1)}, f32[2,256,1]{2,1,0:T(8,128)S(1)}, u32[]{:S(2)}, u32[]{:S(2)}) collective-permute-start(f32[2,256,1]{2,1,0:T(8,128)S(1)} %get-tuple-element.89), channel_id=1, source_target_pairs={{0,16},{16,32},{32,48},{48,64},{64,80},{80,96},{96,112},{1,17},{17... | collective-permute-start | bytes 6152 | tf_op jit(solution)/shard_map/ppermute | solution.py:25
  351.0 7.4 %collective-permute-start.59 = (f32[2,1,258]{2,1,0:T(1,128)S(1)}, f32[2,1,258]{2,1,0:T(1,128)S(1)}, u32[]{:S(2)}, u32[]{:S(2)}) collective-permute-start(f32[2,1,258]{2,1,0:T(1,128)S(1)} %get-tuple-element.37), channel_id=1, source_target_pairs={{1,0},{2,1},{3,2},{4,3},{5,4},{6,5},{7,6},{8,7},{9,8},{10,9},{11,1... | collective-permute-start | bytes 6200 | tf_op jit(solution)/shard_map/ppermute | solution.py:27
  352.3 6.9 %collective-permute-start.58 = (f32[2,1,258]{2,1,0:T(1,128)S(1)}, f32[2,1,258]{2,1,0:T(1,128)S(1)}, u32[]{:S(2)}, u32[]{:S(2)}) collective-permute-start(f32[2,1,258]{2,1,0:T(1,128)S(1)} %get-tuple-element.38), channel_id=1, source_target_pairs={{0,1},{1,2},{2,3},{3,4},{4,5},{5,6},{6,7},{7,8},{8,9},{9,10},{10,1... | collective-permute-start | bytes 6200 | tf_op jit(solution)/shard_map/ppermute | solution.py:25
  361.7 10.8 %collective-permute-start.61 = (f32[2,256,1]{2,1,0:T(8,128)S(1)}, f32[2,256,1]{2,1,0:T(8,128)S(1)}, u32[]{:S(2)}, u32[]{:S(2)}) collective-permute-start(f32[2,256,1]{2,1,0:T(8,128)S(1)} %get-tuple-element.88), channel_id=1, source_target_pairs={{16,0},{32,16},{48,32},{64,48},{80,64},{96,80},{112,96},{17,1},{33... | collective-permute-start | bytes 6152 | tf_op jit(solution)/shard_map/ppermute | solution.py:27
  363.0 11.0 %collective-permute-start.60 = (f32[2,256,1]{2,1,0:T(8,128)S(1)}, f32[2,256,1]{2,1,0:T(8,128)S(1)}, u32[]{:S(2)}, u32[]{:S(2)}) collective-permute-start(f32[2,256,1]{2,1,0:T(8,128)S(1)} %get-tuple-element.87), channel_id=1, source_target_pairs={{0,16},{16,32},{32,48},{48,64},{64,80},{80,96},{96,112},{1,17},{17... | collective-permute-start | bytes 6152 | tf_op jit(solution)/shard_map/ppermute | solution.py:25
  374.1 9.8 %collective-permute-start.63 = (f32[2,1,258]{2,1,0:T(1,128)S(1)}, f32[2,1,258]{2,1,0:T(1,128)S(1)}, u32[]{:S(2)}, u32[]{:S(2)}) collective-permute-start(f32[2,1,258]{2,1,0:T(1,128)S(1)} %get-tuple-element.35), channel_id=1, source_target_pairs={{1,0},{2,1},{3,2},{4,3},{5,4},{6,5},{7,6},{8,7},{9,8},{10,9},{11,1... | collective-permute-start | bytes 6200 | tf_op jit(solution)/shard_map/ppermute | solution.py:27
  375.4 9.2 %collective-permute-start.62 = (f32[2,1,258]{2,1,0:T(1,128)S(1)}, f32[2,1,258]{2,1,0:T(1,128)S(1)}, u32[]{:S(2)}, u32[]{:S(2)}) collective-permute-start(f32[2,1,258]{2,1,0:T(1,128)S(1)} %get-tuple-element.36), channel_id=1, source_target_pairs={{0,1},{1,2},{2,3},{3,4},{4,5},{5,6},{6,7},{7,8},{8,9},{9,10},{10,1... | collective-permute-start | bytes 6200 | tf_op jit(solution)/shard_map/ppermute | solution.py:25
  387.0 10.8 %collective-permute-start.65 = (f32[2,256,1]{2,1,0:T(8,128)S(1)}, f32[2,256,1]{2,1,0:T(8,128)S(1)}, u32[]{:S(2)}, u32[]{:S(2)}) collective-permute-start(f32[2,256,1]{2,1,0:T(8,128)S(1)} %get-tuple-element.86), channel_id=1, source_target_pairs={{16,0},{32,16},{48,32},{64,48},{80,64},{96,80},{112,96},{17,1},{33... | collective-permute-start | bytes 6152 | tf_op jit(solution)/shard_map/ppermute | solution.py:27
  388.3 11.0 %collective-permute-start.64 = (f32[2,256,1]{2,1,0:T(8,128)S(1)}, f32[2,256,1]{2,1,0:T(8,128)S(1)}, u32[]{:S(2)}, u32[]{:S(2)}) collective-permute-start(f32[2,256,1]{2,1,0:T(8,128)S(1)} %get-tuple-element.85), channel_id=1, source_target_pairs={{0,16},{16,32},{32,48},{48,64},{64,80},{80,96},{96,112},{1,17},{17... | collective-permute-start | bytes 6152 | tf_op jit(solution)/shard_map/ppermute | solution.py:25
  399.4 9.6 %collective-permute-start.66 = (f32[2,1,258]{2,1,0:T(1,128)S(1)}, f32[2,1,258]{2,1,0:T(1,128)S(1)}, u32[]{:S(2)}, u32[]{:S(2)}) collective-permute-start(f32[2,1,258]{2,1,0:T(1,128)S(1)} %get-tuple-element.34), channel_id=1, source_target_pairs={{0,1},{1,2},{2,3},{3,4},{4,5},{5,6},{6,7},{7,8},{8,9},{9,10},{10,1... | collective-permute-start | bytes 6200 | tf_op jit(solution)/shard_map/ppermute | solution.py:25
  407.1 9.7 %collective-permute-start.67 = (f32[2,1,258]{2,1,0:T(1,128)S(1)}, f32[2,1,258]{2,1,0:T(1,128)S(1)}, u32[]{:S(2)}, u32[]{:S(2)}) collective-permute-start(f32[2,1,258]{2,1,0:T(1,128)S(1)} %get-tuple-element.33), channel_id=1, source_target_pairs={{1,0},{2,1},{3,2},{4,3},{5,4},{6,5},{7,6},{8,7},{9,8},{10,9},{11,1... | collective-permute-start | bytes 6200 | tf_op jit(solution)/shard_map/ppermute | solution.py:27
  (21 other events, 615.4 us)
Sparse Core Ops, SparseCore 0:
  14.8 49.5 all-gather.4
  434.5 189.2 all-reduce.2
